TPU v7x, 512 devices: a whole 4x8x8 slice. The times are simulated.
512 devices in a mesh: dp: 64 (over x, y, core), code: 8 (over z).
Axes of the slice: x: 4, y: 8, z: 8, core: 2. Of those that a mesh axis runs over, the one named last changes fastest.
Arguments:
- items: float32 [65536, 512], P(('dp', 'code')), may hold values from -6 to 6
- codewords: float32 [8192, 512], P('code'), may hold values from -6 to 6
- assign: int32 [65536], P('dp'), may hold values from 0 to 8191, as said below
Outputs:
- new_codewords: float32 [8192, 512], P('code', 'dp')
- residual: float32 [65536, 512], P(('dp', 'code'))
Inputs may be any that keep to these rules, and one draw needn't show every extreme that they name: `assign`: the items are laid out in aligned blocks of 128 (the items of one device). Splitting the codewords into equal ranges, one per index of code, the items of one block name codewords of exactly half of the ranges, 32 items for each such range.
All inputs are finite; a program needn't handle non-finite values.
Results may differ from a plain program's by a relative error of at most 0.0003.
Values sent between devices are 32-bit elements; how exact they have to be, the bound alone decides.
No kernel may reach another device: no remote copies, remote signals or barrier semaphores. Data moves between devices by JAX's collectives and lax.ppermute only.
A program may use at most 64 MiB of HBM per device.

v0:
```python
import jax
import jax.numpy as jnp
from jax import lax
from jax.sharding import PartitionSpec as P

K = 8192
ITERS = 3
epsilon = 1e-05
inverse_temp = 64.0


def unit_rows(values):
    return values * lax.rsqrt(jnp.mean(values * values, axis=-1, keepdims=True) + epsilon)


def kernel_of(rows_block, scaled):
    return jnp.exp(
        jnp.dot(
            unit_rows(rows_block),
            scaled.T,
            precision=lax.Precision.HIGHEST,
            preferred_element_type=jnp.float32,
        )
    )


def column_scale(col_part):
    summed = lax.psum(col_part, "dp")
    return 1.0 / (K * summed)


def row_scaling(row_part, total_items):
    summed = lax.psum(row_part, "code")
    return 1.0 / (total_items * summed)


def body(items, codewords, assign):
    code_count = lax.axis_size("code")
    dp_count = lax.axis_size("dp")
    local_codes = codewords.shape[0]
    width = items.shape[1]
    own_rows = items.shape[0]
    total_items = own_rows * code_count * dp_count
    scaled = unit_rows(codewords) * (inverse_temp / width)
    gathered = lax.all_gather(items, "code", axis=0, tiled=True)
    kernel_vals = kernel_of(gathered, scaled)
    col_part = jnp.sum(kernel_vals, axis=0)
    row_scale = jnp.ones((kernel_vals.shape[0],), jnp.float32)
    for sweep_index in range(ITERS):
        col_scale = column_scale(col_part)
        row_part = jnp.dot(
            kernel_vals,
            col_scale,
            precision=lax.Precision.HIGHEST,
            preferred_element_type=jnp.float32,
        )
        row_scale = row_scaling(row_part, total_items)
        col_part = jnp.dot(
            row_scale,
            kernel_vals,
            precision=lax.Precision.HIGHEST,
            preferred_element_type=jnp.float32,
        )
    mass = lax.psum(col_part, "dp")
    numerator = lax.dot_general(
        kernel_vals,
        row_scale[:, None] * gathered,
        (((0,), (0,)), ((), ())),
        precision=lax.Precision.HIGHEST,
        preferred_element_type=jnp.float32,
    )
    owned_sums = lax.psum_scatter(numerator, "dp", scatter_dimension=1, tiled=True)
    new_codewords = owned_sums / mass[:, None]
    my_code = lax.axis_index("code")
    offset = my_code * local_codes
    index_rows = assign - offset
    inside = (index_rows >= 0) & (index_rows < local_codes)
    picked = jnp.take(codewords, jnp.clip(index_rows, 0, local_codes - 1), axis=0)
    looked = lax.psum_scatter(
        jnp.where(inside[:, None], picked, jnp.float32(0.0)),
        "code",
        scatter_dimension=0,
        tiled=True,
    )
    residual = items - looked
    return (new_codewords, residual)


def solution(mesh):
    in_specs = (P(("dp", "code"), None), P("code", None), P("dp"))
    out_specs = (P("code", "dp"), P(("dp", "code"), None))
    return jax.shard_map(body, mesh=mesh, in_specs=in_specs, out_specs=out_specs, check_vma=False)
```

profile of v0, /device:TPU:16, one launch (start us, length us, event | category | flops | bytes accessed | tf_op | source)
XLA Modules:
  0.0 675.3 jit_solution(14707872022729318664)
XLA Ops:
  7.2 0.0 all-gather.2.cloned.1.call-start
  7.2 0.7 all-gather.2.cloned.1.call-update
  7.9 0.0 reduce-scatter.5.cloned.1.call-start
  7.9 0.7 fusion.23
  8.6 5.6 gather_fusion
  14.3 2.0 select_select_fusion
  16.3 0.0 reduce-scatter.5.cloned.1.call-update
  16.3 0.0 reduce-scatter.3.cloned.1.call-start
  16.4 1.5 copy-done
  17.9 0.2 multiply_reduce_fusion
  18.1 41.1 %all-gather.2.cloned.1.call-done = f32[1024,512]{1,0:T(8,128)} async-done(((f32[128,512]{1,0:T(8,128)}), f32[1024,512]{1,0:T(8,128)}) %all-gather.2.cloned.1.call-update) | async-done | bytes 2097168 | tf_op jit(solution)/shard_map/all_gather | solution.py:45
  59.2 2.0 multiply_reduce_fusion.1
  61.2 0.3 copy-done.1
  61.5 9.1 %exponential_reduce_fusion = (f32[1024]{0:T(1024)S(1)}, f32[1024,1024]{1,0:T(8,128)}) fusion(f32[1024,512]{1,0:T(8,128)S(1)} %copy-done, f32[1024]{0:T(1024)S(1)} %add_rsqrt_fusion, f32[1024,512]{1,0:T(8,128)S(1)} %copy-done.1, f32[1024]{0:T(1024)S(1)} %add_rsqrt_fusion.1), kind=kOutput, calls=%fused_computation.15 | convolution fusion | flops 6445071360 | bytes 8400896 | tf_op jit(solution)/shard_map/dot_general | solution.py:18
  70.5 114.3 %psum.49 = f32[1024]{0:T(1024)S(1)} all-reduce(f32[1024]{0:T(1024)S(1)} %get-tuple-element.4), channel_id=1, replica_groups=mesh['dp'=64,'code'=8] {'dp'}, use_global_device_ids=true, to_apply=%region_3.0 | all-reduce | flops 1024 | bytes 8192 | tf_op jit(solution)/shard_map/psum | solution.py:28
  184.8 6.2 fusion.12
  191.0 16.1 %psum.50 = f32[1024]{0:T(1024)S(1)} all-reduce(f32[1024]{0:T(1024)S(1)} %bitcast.21), channel_id=1, replica_groups=mesh['dp'=64,'code'=8] {'code'}, use_global_device_ids=true, to_apply=%region_4.0 | all-reduce | flops 1024 | bytes 8192 | tf_op jit(solution)/shard_map/psum | solution.py:33
  207.1 4.5 fusion.10
  211.6 124.2 %psum.51 = f32[1024]{0:T(1024)S(1)} all-reduce(f32[1024]{0:T(1024)S(1)} %bitcast.23), channel_id=1, replica_groups=mesh['dp'=64,'code'=8] {'dp'}, use_global_device_ids=true, to_apply=%region_5.0 | all-reduce | flops 1024 | bytes 8192 | tf_op jit(solution)/shard_map/psum | solution.py:28
  335.8 6.2 fusion.8
  342.0 14.2 %psum.52 = f32[1024]{0:T(1024)S(1)} all-reduce(f32[1024]{0:T(1024)S(1)} %bitcast.25), channel_id=1, replica_groups=mesh['dp'=64,'code'=8] {'code'}, use_global_device_ids=true, to_apply=%region_6.0 | all-reduce | flops 1024 | bytes 8192 | tf_op jit(solution)/shard_map/psum | solution.py:33
  356.2 4.5 fusion.6
  360.7 124.0 %psum.53 = f32[1024]{0:T(1024)S(1)} all-reduce(f32[1024]{0:T(1024)S(1)} %bitcast.27), channel_id=1, replica_groups=mesh['dp'=64,'code'=8] {'dp'}, use_global_device_ids=true, to_apply=%region_7.0 | all-reduce | flops 1024 | bytes 8192 | tf_op jit(solution)/shard_map/psum | solution.py:28
  484.7 6.3 fusion.4
  491.1 16.4 %psum.54 = f32[1024]{0:T(1024)S(1)} all-reduce(f32[1024]{0:T(1024)S(1)} %bitcast.29), channel_id=1, replica_groups=mesh['dp'=64,'code'=8] {'code'}, use_global_device_ids=true, to_apply=%region_8.0 | all-reduce | flops 1024 | bytes 8192 | tf_op jit(solution)/shard_map/psum | solution.py:33
  507.5 10.3 %fusion.2 = f32[1024,512]{0,1:T(8,128)} fusion(f32[1024,1024]{1,0:T(8,128)} %get-tuple-element.5, f32[1024,512]{1,0:T(8,128)S(1)} %copy-done.2, f32[1024]{0:T(1024)S(1)} %multiply_divide_fusion), kind=kOutput, calls=%fused_computation.3 | convolution fusion | flops 6442975232 | bytes 8392704 | tf_op jit(solution)/shard_map/dot_general | solution.py:65
  517.8 0.0 reduce-scatter.3.cloned.1.call-update
  517.8 4.5 fusion
  522.4 124.2 %psum.55 = f32[1024]{0:T(1024)S(1)} all-reduce(f32[1024]{0:T(1024)S(1)} %bitcast.20), channel_id=1, replica_groups=mesh['dp'=64,'code'=8] {'dp'}, use_global_device_ids=true, to_apply=%region_10.0 | all-reduce | flops 1024 | bytes 8192 | tf_op jit(solution)/shard_map/psum | solution.py:64
  646.6 1.7 sub.11
  648.3 19.1 %reduce-scatter.3.cloned.1.call-done = f32[1024,8]{0,1:T(8,128)} async-done(((f32[1024,512]{0,1:T(8,128)}), f32[1024,8]{0,1:T(8,128)}) %reduce-scatter.3.cloned.1.call-update) | async-done | bytes 32784 | tf_op jit(solution)/shard_map/reduce_scatter | solution.py:72
  667.4 1.4 broadcast_divide_fusion
  (18 shorter events, 0.1 us)
Async XLA Ops:
  7.2 52.1 %all-gather.2.cloned.1.call-start = ((), (), s32[]{:S(2)}) async-start(), calls=%async_computation.2 | async-start | bytes 2359296 | tf_op jit(solution)/shard_map/all_gather | solution.py:45
  7.9 638.7 %reduce-scatter.5.cloned.1.call-start = ((), (), s32[]{:S(2)}) async-start(), calls=%async_computation.4 | async-start | bytes 2359296 | tf_op jit(solution)/shard_map/reduce_scatter | solution.py:79
  8.6 5.6 copy-start.4
  16.3 1.6 copy-start
  16.3 651.1 %reduce-scatter.3.cloned.1.call-start = ((), (), s32[]{:S(2)}) async-start(), calls=%async_computation.3 | async-start | bytes 2129920 | tf_op jit(solution)/shard_map/reduce_scatter | solution.py:72
  59.2 2.2 copy-start.1
  484.7 22.7 %copy-start.2 = (f32[1024,512]{1,0:T(8,128)S(1)}, f32[1024,512]{1,0:T(8,128)}, u32[]{:S(2)}) copy-start(f32[1024,512]{1,0:T(8,128)} %all-gather.2.cloned.1.call-done) | copy-start | bytes 6291460
  517.8 128.8 %copy-start.3 = (f32[128,512]{1,0:T(8,128)S(1)}, f32[128,512]{1,0:T(8,128)}, u32[]{:S(2)}) copy-start(f32[128,512]{1,0:T(8,128)} %param.3) | copy-start | bytes 786436
Sparse Core Ops, SparseCore 0:
  10.1 49.1 all-gather.1
  62.1 43.7 reduce-scatter.4
  517.9 149.3 reduce-scatter.2
where the time goes:
time: 676 us; the launch traced here: 675 us
  blocking collectives  533 us (79%)
  waiting for transfers between devices  60.9 us (9%)
  matrix products  51.6 us (8%)
  between operations  13.9 us (2%)
  other arithmetic  7.99 us (1%)
  local copies, waits for them, and re-layouts  7.4 us (1%)
    psum x3, blocking collectives, column_scale(): summed = lax.psum(col_part, 'dp')  363 us
    psum x1, blocking collectives, body(): mass = lax.psum(col_part, 'dp')  124 us
    psum x3, blocking collectives, row_scaling(): summed = lax.psum(row_part, 'code')  46.7 us
    all_gather x1, waiting for transfers between devices, body(): gathered = lax.all_gather(items, 'code', axis=0, tiled=True)  41.1 us
    reduce_scatter x1, waiting for transfers between devices, body(): lax.psum_scatter(numerator, 'dp', scatter_dimension=1, tiled=True)  19.1 us
    dot_general x3, matrix products, body(): jnp.dot(kernel_vals, col_scale, precision=lax.Precision.HIGHEST, preferre...  18.7 us
  transfers between devices with their start and end apart: 3, of which 2 were waited for; matrix products, arithmetic and copies ran while one was open for 9% of the time, Pallas kernels for 0%

commit v1 on v0

--- a/solution.py
+++ b/solution.py
@@ -42,7 +42,12 @@
     own_rows = items.shape[0]
     total_items = own_rows * code_count * dp_count
     scaled = unit_rows(codewords) * (inverse_temp / width)
-    gathered = lax.all_gather(items, "code", axis=0, tiled=True)
+    ring = [items]
+    for hop in range(7):
+        ring.append(lax.ppermute(ring[-1], "code", [(dev, (dev + 1) % 8) for dev in range(8)]))
+    gathered = jnp.roll(
+        jnp.concatenate(ring[::-1], axis=0), (lax.axis_index("code") + 1) * ring[0].shape[0], axis=0
+    )
     kernel_vals = kernel_of(gathered, scaled)
     col_part = jnp.sum(kernel_vals, axis=0)
     row_scale = jnp.ones((kernel_vals.shape[0],), jnp.float32)

time: 676 us -> 741 us (1.096)
  waiting for transfers between devices: 60.9 us -> 94.1 us
  starting transfers between devices: 0.12 us -> 15.8 us
  local copies, waits for them, and re-layouts: 7.4 us -> 21.6 us
    ppermute x0 -> x7, waiting for transfers between devices: none -> 72.6 us  [body(): lax.ppermute(ring[-1], 'code', [(dev, (dev + 1) % 8) for dev in range(8)])]
    all_gather x1 -> x0, waiting for transfers between devices: 41.1 us -> none  [body(): gathered = lax.all_gather(items, 'code', axis=0, tiled=True)]
    ppermute x0 -> x7, starting transfers between devices: none -> 15.7 us  [body(): lax.ppermute(ring[-1], 'code', [(dev, (dev + 1) % 8) for dev in range(8)])]
    unnamed x10 -> x20, local copies, waits for them, and re-layouts: 1.78 us -> 13.9 us
  transfers between devices with their start and end apart: 3 -> 9, of which waited for: 2 -> 8; matrix products, arithmetic and copies ran while one was open for 9% -> 2% of each run, Pallas kernels for 0% -> 0%
where the time goes in v1:
time: 741 us; the launch traced here: 740 us
  blocking collectives  532 us (72%)
  waiting for transfers between devices  94.1 us (13%)
  matrix products  52.9 us (7%)
  local copies, waits for them, and re-layouts  21.6 us (3%)
  starting transfers between devices  15.8 us (2%)
  between operations  14.2 us (2%)
  other arithmetic  10.1 us (1%)
    psum x3, blocking collectives, column_scale(): summed = lax.psum(col_part, 'dp')  363 us
    psum x1, blocking collectives, body(): mass = lax.psum(col_part, 'dp')  124 us
    ppermute x7, waiting for transfers between devices, body(): lax.ppermute(ring[-1], 'code', [(dev, (dev + 1) % 8) for dev in range(8)])  72.6 us
    psum x3, blocking collectives, row_scaling(): summed = lax.psum(row_part, 'code')  44.7 us
    reduce_scatter x1, waiting for transfers between devices, body(): lax.psum_scatter(numerator, 'dp', scatter_dimension=1, tiled=True)  21.4 us
    dot_general x3, matrix products, body(): jnp.dot(kernel_vals, col_scale, precision=lax.Precision.HIGHEST, preferre...  18.5 us
    ppermute x7, starting transfers between devices, body(): lax.ppermute(ring[-1], 'code', [(dev, (dev + 1) % 8) for dev in range(8)])  15.7 us
  transfers between devices with their start and end apart: 9, of which 8 were waited for; matrix products, arithmetic and copies ran while one was open for 2% of the time, Pallas kernels for 0%

profile of v1, /device:TPU:16, one launch (start us, length us, event | category | flops | bytes accessed | tf_op | source)
XLA Modules:
  0.0 740.5 jit_solution(16304761518974999298)
XLA Ops:
  8.6 6.9 gather_fusion
  15.5 3.3 select_select_fusion
  18.9 4.3 collective-permute-start
  23.2 13.0 %collective-permute-done = f32[128,512]{1,0:T(8,128)S(1)} collective-permute-done((f32[128,512]{1,0:T(8,128)S(1)}, f32[128,512]{1,0:T(8,128)S(1)}, u32[]{:S(2)}, u32[]{:S(2)}) %collective-permute-start) | collective-permute-done | bytes 262176 | tf_op jit(solution)/shard_map/ppermute | solution.py:47
  36.2 1.9 collective-permute-start.1
  38.1 14.7 %collective-permute-done.1 = f32[128,512]{1,0:T(8,128)S(1)} collective-permute-done((f32[128,512]{1,0:T(8,128)S(1)}, f32[128,512]{1,0:T(8,128)S(1)}, u32[]{:S(2)}, u32[]{:S(2)}) %collective-permute-start.1) | collective-permute-done | bytes 262176 | tf_op jit(solution)/shard_map/ppermute | solution.py:47
  52.8 1.9 collective-permute-start.2
  54.7 14.4 %collective-permute-done.2 = f32[128,512]{1,0:T(8,128)S(1)} collective-permute-done((f32[128,512]{1,0:T(8,128)S(1)}, f32[128,512]{1,0:T(8,128)S(1)}, u32[]{:S(2)}, u32[]{:S(2)}) %collective-permute-start.2) | collective-permute-done | bytes 262176 | tf_op jit(solution)/shard_map/ppermute | solution.py:47
  69.1 1.9 collective-permute-start.3
  71.0 7.5 %collective-permute-done.3 = f32[128,512]{1,0:T(8,128)S(1)} collective-permute-done((f32[128,512]{1,0:T(8,128)S(1)}, f32[128,512]{1,0:T(8,128)S(1)}, u32[]{:S(2)}, u32[]{:S(2)}) %collective-permute-start.3) | collective-permute-done | bytes 262176 | tf_op jit(solution)/shard_map/ppermute | solution.py:47
  78.6 1.9 collective-permute-start.4
  80.5 7.5 %collective-permute-done.4 = f32[128,512]{1,0:T(8,128)S(1)} collective-permute-done((f32[128,512]{1,0:T(8,128)S(1)}, f32[128,512]{1,0:T(8,128)S(1)}, u32[]{:S(2)}, u32[]{:S(2)}) %collective-permute-start.4) | collective-permute-done | bytes 262176 | tf_op jit(solution)/shard_map/ppermute | solution.py:47
  88.1 1.9 collective-permute-start.5
  90.0 7.8 %collective-permute-done.5 = f32[128,512]{1,0:T(8,128)} collective-permute-done((f32[128,512]{1,0:T(8,128)S(1)}, f32[128,512]{1,0:T(8,128)}, u32[]{:S(2)}, u32[]{:S(2)}) %collective-permute-start.5) | collective-permute-done | bytes 262176 | tf_op jit(solution)/shard_map/ppermute | solution.py:47
  97.8 1.9 collective-permute-start.6
  100.0 7.6 %collective-permute-done.6 = f32[128,512]{1,0:T(8,128)} collective-permute-done((f32[128,512]{1,0:T(8,128)}, f32[128,512]{1,0:T(8,128)}, u32[]{:S(2)}, u32[]{:S(2)}) %collective-permute-start.6) | collective-permute-done | bytes 262176 | tf_op jit(solution)/shard_map/ppermute | solution.py:47
  126.0 10.0 %exponential_reduce_fusion = (f32[1024]{0:T(1024)S(1)}, f32[1024,1024]{1,0:T(8,128)}) fusion(f32[1024,512]{1,0:T(8,128)S(1)} %copy-done, f32[1024]{0:T(1024)S(1)} %add_rsqrt_fusion, f32[2048,512]{1,0:T(8,128)} %constant_dynamic-update-slice_fusion, s32[]{:T(128)S(6)} %select_n.27, f32[1024]{0:T(1024)S(1)} %add_rsqrt_fusion.1), kind=kOutput, calls=%fused_computation.15 | convolution fusion | flops 6445071360 | bytes 8400900 | tf_op jit(solution)/shard_map/dot_general | solution.py:18
  136.0 114.7 %psum.49 = f32[1024]{0:T(1024)S(1)} all-reduce(f32[1024]{0:T(1024)S(1)} %get-tuple-element.6), channel_id=1, replica_groups=mesh['dp'=64,'code'=8] {'dp'}, use_global_device_ids=true, to_apply=%region_3.4 | all-reduce | flops 1024 | bytes 8192 | tf_op jit(solution)/shard_map/psum | solution.py:28
  250.6 6.2 fusion.12
  256.8 14.2 %psum.50 = f32[1024]{0:T(1024)S(1)} all-reduce(f32[1024]{0:T(1024)S(1)} %bitcast.21), channel_id=1, replica_groups=mesh['dp'=64,'code'=8] {'code'}, use_global_device_ids=true, to_apply=%region_4.5 | all-reduce | flops 1024 | bytes 8192 | tf_op jit(solution)/shard_map/psum | solution.py:33
  271.0 4.5 fusion.10
  275.5 124.2 %psum.51 = f32[1024]{0:T(1024)S(1)} all-reduce(f32[1024]{0:T(1024)S(1)} %bitcast.23), channel_id=1, replica_groups=mesh['dp'=64,'code'=8] {'dp'}, use_global_device_ids=true, to_apply=%region_5.6 | all-reduce | flops 1024 | bytes 8192 | tf_op jit(solution)/shard_map/psum | solution.py:28
  399.7 6.2 fusion.8
  405.9 16.2 %psum.52 = f32[1024]{0:T(1024)S(1)} all-reduce(f32[1024]{0:T(1024)S(1)} %bitcast.25), channel_id=1, replica_groups=mesh['dp'=64,'code'=8] {'code'}, use_global_device_ids=true, to_apply=%region_6.7 | all-reduce | flops 1024 | bytes 8192 | tf_op jit(solution)/shard_map/psum | solution.py:33
  422.0 4.5 fusion.6
  426.5 124.0 %psum.53 = f32[1024]{0:T(1024)S(1)} all-reduce(f32[1024]{0:T(1024)S(1)} %bitcast.27), channel_id=1, replica_groups=mesh['dp'=64,'code'=8] {'dp'}, use_global_device_ids=true, to_apply=%region_7.8 | all-reduce | flops 1024 | bytes 8192 | tf_op jit(solution)/shard_map/psum | solution.py:28
  550.6 6.2 fusion.4
  556.7 14.4 %psum.54 = f32[1024]{0:T(1024)S(1)} all-reduce(f32[1024]{0:T(1024)S(1)} %bitcast.29), channel_id=1, replica_groups=mesh['dp'=64,'code'=8] {'code'}, use_global_device_ids=true, to_apply=%region_8.9 | all-reduce | flops 1024 | bytes 8192 | tf_op jit(solution)/shard_map/psum | solution.py:33
  571.1 11.0 %fusion.2 = f32[1024,512]{0,1:T(8,128)} fusion(f32[1024,1024]{1,0:T(8,128)} %get-tuple-element.7, f32[2048,512]{1,0:T(8,128)} %constant_dynamic-update-slice_fusion, s32[]{:T(128)S(6)} %select_n.27, f32[1024]{0:T(1024)S(1)} %multiply_divide_fusion), kind=kOutput, calls=%fused_computation.3 | convolution fusion | flops 6442975232 | bytes 8392708 | tf_op jit(solution)/shard_map/dot_general | solution.py:70
  582.1 4.5 fusion
  586.6 124.2 %psum.55 = f32[1024]{0:T(1024)S(1)} all-reduce(f32[1024]{0:T(1024)S(1)} %bitcast.20), channel_id=1, replica_groups=mesh['dp'=64,'code'=8] {'dp'}, use_global_device_ids=true, to_apply=%region_10.11 | all-reduce | flops 1024 | bytes 8192 | tf_op jit(solution)/shard_map/psum | solution.py:69
  710.8 21.4 %reduce-scatter.3.cloned.1.call-done = f32[1024,8]{0,1:T(8,128)} async-done(((f32[1024,512]{0,1:T(8,128)}), f32[1024,8]{0,1:T(8,128)}) %reduce-scatter.3.cloned.1.call-update) | async-done | bytes 32784 | tf_op jit(solution)/shard_map/reduce_scatter | solution.py:77
  (40 shorter events, 21.5 us)
Async XLA Ops:
  7.2 107.4 %reduce-scatter.5.cloned.1.call-start = ((), (), s32[]{:S(2)}) async-start(), calls=%async_computation.3 | async-start | bytes 2359296 | tf_op jit(solution)/shard_map/reduce_scatter | solution.py:84
  15.5 3.4 copy-start.1
  15.5 84.2 %copy-start = (f32[1024,512]{1,0:T(8,128)S(1)}, f32[1024,512]{1,0:T(8,128)}, u32[]{:S(2)}) copy-start(f32[1024,512]{1,0:T(8,128)} %param.4) | copy-start | bytes 6291460
  18.9 713.4 %reduce-scatter.3.cloned.1.call-start = ((), (), s32[]{:S(2)}) async-start(), calls=%async_computation.2 | async-start | bytes 2129920 | tf_op jit(solution)/shard_map/reduce_scatter | solution.py:77
  18.9 17.2 %collective-permute-start = (f32[128,512]{1,0:T(8,128)S(1)}, f32[128,512]{1,0:T(8,128)S(1)}, u32[]{:S(2)}, u32[]{:S(2)}) collective-permute-start(f32[128,512]{1,0:T(8,128)S(1)} %copy-done.1), channel_id=1, source_target_pairs={{0,1},{1,2},{2,3},{3,4},{4,5},{5,6},{6,7},{7,0},{8,9},{9,10},{10,1... | collective-permute-start | bytes 786440 | tf_op jit(solution)/shard_map/ppermute | solution.py:47
  36.2 16.6 %collective-permute-start.1 = (f32[128,512]{1,0:T(8,128)S(1)}, f32[128,512]{1,0:T(8,128)S(1)}, u32[]{:S(2)}, u32[]{:S(2)}) collective-permute-start(f32[128,512]{1,0:T(8,128)S(1)} %collective-permute-done), channel_id=1, source_target_pairs={{0,1},{1,2},{2,3},{3,4},{4,5},{5,6},{6,7},{7,0},{8,9},{9,10},{10,1... | collective-permute-start | bytes 786440 | tf_op jit(solution)/shard_map/ppermute | solution.py:47
  52.8 16.4 %collective-permute-start.2 = (f32[128,512]{1,0:T(8,128)S(1)}, f32[128,512]{1,0:T(8,128)S(1)}, u32[]{:S(2)}, u32[]{:S(2)}) collective-permute-start(f32[128,512]{1,0:T(8,128)S(1)} %collective-permute-done.1), channel_id=1, source_target_pairs={{0,1},{1,2},{2,3},{3,4},{4,5},{5,6},{6,7},{7,0},{8,9},{9,10},{10,1... | collective-permute-start | bytes 786440 | tf_op jit(solution)/shard_map/ppermute | solution.py:47
  69.1 9.5 %collective-permute-start.3 = (f32[128,512]{1,0:T(8,128)S(1)}, f32[128,512]{1,0:T(8,128)S(1)}, u32[]{:S(2)}, u32[]{:S(2)}) collective-permute-start(f32[128,512]{1,0:T(8,128)S(1)} %collective-permute-done.2), channel_id=1, source_target_pairs={{0,1},{1,2},{2,3},{3,4},{4,5},{5,6},{6,7},{7,0},{8,9},{9,10},{10,1... | collective-permute-start | bytes 786440 | tf_op jit(solution)/shard_map/ppermute | solution.py:47
  78.6 9.5 %collective-permute-start.4 = (f32[128,512]{1,0:T(8,128)S(1)}, f32[128,512]{1,0:T(8,128)S(1)}, u32[]{:S(2)}, u32[]{:S(2)}) collective-permute-start(f32[128,512]{1,0:T(8,128)S(1)} %collective-permute-done.3), channel_id=1, source_target_pairs={{0,1},{1,2},{2,3},{3,4},{4,5},{5,6},{6,7},{7,0},{8,9},{9,10},{10,1... | collective-permute-start | bytes 786440 | tf_op jit(solution)/shard_map/ppermute | solution.py:47
  88.1 9.7 %collective-permute-start.5 = (f32[128,512]{1,0:T(8,128)S(1)}, f32[128,512]{1,0:T(8,128)}, u32[]{:S(2)}, u32[]{:S(2)}) collective-permute-start(f32[128,512]{1,0:T(8,128)S(1)} %collective-permute-done.4), channel_id=1, source_target_pairs={{0,1},{1,2},{2,3},{3,4},{4,5},{5,6},{6,7},{7,0},{8,9},{9,10},{10,1... | collective-permute-start | bytes 786440 | tf_op jit(solution)/shard_map/ppermute | solution.py:47
  97.8 9.8 %collective-permute-start.6 = (f32[128,512]{1,0:T(8,128)}, f32[128,512]{1,0:T(8,128)}, u32[]{:S(2)}, u32[]{:S(2)}) collective-permute-start(f32[128,512]{1,0:T(8,128)} %collective-permute-done.5), channel_id=1, source_target_pairs={{0,1},{1,2},{2,3},{3,4},{4,5},{5,6},{6,7},{7,0},{8,9},{9,10},{10,1... | collective-permute-start | bytes 786440 | tf_op jit(solution)/shard_map/ppermute | solution.py:47
  114.5 8.9 %copy-start.2 = (f32[128,512]{1,0:T(8,128)S(1)}, f32[128,512]{1,0:T(8,128)}, u32[]{:S(2)}) copy-start(f32[128,512]{1,0:T(8,128)} %param.3) | copy-start | bytes 786436
Sparse Core Ops, SparseCore 0:
  19.0 55.6 reduce-scatter.4
  582.2 149.9 reduce-scatter.2
